TPU v7x, 32 devices: a whole 2x2x4 slice. The times are simulated.
32 devices in a mesh: group: 2 (over y), rows: 4 (over z), sec: 2 (over x), sub: 2 (over core).
Axes of the slice: x: 2, y: 2, z: 4, core: 2. Of those that a mesh axis runs over, the one named last changes fastest.
Arguments:
- row_seeds: int32 [16384], P(('group', 'rows')), parts along dimension 0, may hold values from 0 to 65520
- labels: int32 [16384], P(('group', 'rows')), parts along dimension 0, may hold values from 0 to 1
- weights: float32 [131072], P(('group', 'sec', 'sub')), parts along dimension 0, may hold values from -5 to 5
- sketch: bfloat16 [65536, 64], P(('sec', 'sub')), may hold values from -5 to 5
Outputs:
- step: float32 [131072], P(('group', 'sec', 'sub')), parts along dimension 0
- sketched: float32 [131072, 64], P(('group', 'sec', 'sub')), parts along dimension 0
There are 2 independent parts, one for each index of `group`. A program takes and returns all parts, laid end to end along the dimension named above; an argument that names none is the same for every part. Nothing has to cross between parts.
All inputs are finite; a program needn't handle non-finite values.
Results may differ from a plain program's by a relative error of at most 0.0029.
Values may be sent and summed in bfloat16 or wider, within the bound.
No kernel may reach another device: no remote copies, remote signals or barrier semaphores. Data moves between devices by JAX's collectives and lax.ppermute only.
A program may use at most 128 MiB of HBM per device.

v0:
```python
import jax
import jax.numpy as jnp
from jax import lax
from jax.sharding import PartitionSpec as P

ROOT = 256


def table_block(seeds, first, count):
    cols = first + lax.iota(jnp.int32, count)
    part_a = cols * 30011 % 65521
    part_b = seeds * 16411 % 65521
    mixer = (part_b[:, None] + part_a[None, :]) % 65521
    folded = mixer % 46337
    mixer = folded * folded % 65521
    mixer = (mixer * 31 + part_a[None, :] + 7) % 65521
    level = mixer % 16
    return ((level.astype(jnp.float32) - 7.5) * (1.0 / (4.0 * ROOT))).astype(jnp.bfloat16)


def block_size():
    return 512


def margin_rows(seeds, first, stacked):
    count = seeds.shape[0]
    blk = block_size()
    nblk = count // blk
    nfeat = stacked.shape[0]

    def one_block(block_seeds):
        return jnp.dot(
            table_block(block_seeds, first, nfeat), stacked, preferred_element_type=jnp.float32
        )

    return lax.map(one_block, seeds.reshape(nblk, blk)).reshape(count, stacked.shape[1])


def accumulate(seeds, mixed, first, nfeat):
    count = seeds.shape[0]
    blk = block_size()
    nblk = count // blk

    def add_block(index, acc):
        block_seeds = lax.dynamic_slice_in_dim(seeds, index * blk, blk, 0)
        block_mixed = lax.dynamic_slice_in_dim(mixed, index * blk, blk, 0)
        tab = table_block(block_seeds, first, nfeat)
        return acc + lax.dot_general(
            tab, block_mixed, (((0,), (0,)), ((), ())), preferred_element_type=jnp.float32
        )

    return lax.fori_loop(0, nblk, add_block, jnp.zeros((nfeat, mixed.shape[1]), jnp.float32))


def weigh(margins, labels):
    prob = jax.nn.sigmoid(margins[:, 0])
    resid = prob - labels.astype(jnp.float32)
    curv = prob * (1.0 - prob)
    return jnp.concatenate([resid[:, None], curv[:, None] * margins[:, 1:]], axis=1).astype(
        jnp.bfloat16
    )


def products(sketch_part, sketched, grad):
    highest = lax.Precision.HIGHEST
    core = lax.dot_general(
        sketch_part.astype(jnp.float32), sketched, (((0,), (0,)), ((), ())), precision=highest
    )
    square = lax.dot_general(sketched, sketched, (((0,), (0,)), ((), ())), precision=highest)
    proj = lax.dot_general(sketched, grad, (((0,), (0,)), ((), ())), precision=highest)
    return (core, square, proj)


def finish(core, square, proj, sketched, grad, lam):
    inner = lam * core + square
    inner = 0.5 * (inner + inner.T)
    factor = jnp.linalg.cholesky(inner)
    middle = lax.linalg.triangular_solve(factor, proj[:, None], left_side=True, lower=True)
    coef = lax.linalg.triangular_solve(
        factor, middle, left_side=True, lower=True, transpose_a=True
    )[:, 0]
    return (grad - jnp.dot(sketched, coef, precision=lax.Precision.HIGHEST)) / lam


def local(row_seeds, labels, weights, sketch):
    lam = 0.05
    nfeat = weights.shape[0]
    first = lax.axis_index(("sec", "sub")) * nfeat
    stacked = jnp.concatenate([weights.astype(jnp.bfloat16)[:, None], sketch], axis=1)
    local_margins = margin_rows(row_seeds, first, stacked)
    margins = lax.psum(local_margins, ("sec", "sub"))
    mixed = weigh(margins, labels)
    partial_total = accumulate(row_seeds, mixed, first, nfeat)
    piece = lax.psum_scatter(partial_total, "rows", scatter_dimension=0, tiled=True)
    count = piece.shape[0]
    position = lax.axis_index("rows") * count
    own_weights = lax.dynamic_slice_in_dim(weights, position, count, 0)
    own_sketch = lax.dynamic_slice_in_dim(sketch, position, count, 0)
    grad = piece[:, 0] + lam * own_weights
    sketched = piece[:, 1:] + lam * own_sketch.astype(jnp.float32)
    core, square, proj = products(own_sketch, sketched, grad)
    core, square, proj = lax.psum((core, square, proj), ("rows", "sec", "sub"))
    step = finish(core, square, proj, sketched, grad, lam)
    step, sketched = (
        lax.all_gather(step, "rows", axis=0, tiled=True),
        lax.all_gather(sketched, "rows", axis=0, tiled=True),
    )
    return (step, sketched)


def solution(mesh):
    placed = (
        P(("group", "rows")),
        P(("group", "rows")),
        P(("group", "sec", "sub")),
        P(("sec", "sub"), None),
    )
    return jax.shard_map(
        local,
        mesh=mesh,
        in_specs=placed,
        out_specs=(P(("group", "sec", "sub")), P(("group", "sec", "sub"), None)),
        check_vma=False,
    )
```

profile of v0, /device:TPU:0, one launch (start us, length us, event | category | flops | bytes accessed | tf_op | source)
XLA Modules:
  0.0 1060.1 jit_solution(18047026899343946793)
XLA Ops:
  7.2 0.8 convert_element_type.47
  8.1 3.8 broadcast_in_dim.39
  11.9 4.7 copy.29
  16.7 0.7 reshape.76
  17.4 5.9 pad_maximum_fusion
  23.3 415.5 %while.30 = (s32[]{:T(128)}, f32[4,512,65]{1,0,2:T(4,128)S(1)}, s32[4,512]{1,0:T(4,128)S(1)}, s32[]{:T(128)}, bf16[16384,65]{1,0:T(8,128)(2,1)}, /*index=5*/s32[]{:T(128)}, s32[]{:T(128)}) while((s32[]{:T(128)}, f32[4,512,65]{1,0,2:T(4,128)S(1)}, s32[4,512]{1,0:T(4,128)S(1)}, s32[]{:T(128)}, bf16[16384,65]{1,0:T(8,128)(2,1)}, ...), condition=%wide.region_1.2_spmd, body=%wide.region_0.1_spmd.sunk | while | flops 1459752448 | bytes 45011060 | solution.py:36
  23.4 91.7 %fusion.121 = bf16[512,16384]{1,0:T(8,128)(2,1)} fusion(s32[16384]{0:T(1024)S(1)} %add_select_fusion.18, s32[512]{0:T(512)S(1)} %add_select_fusion.19), kind=kLoop, calls=%fused_computation.18.clone.clone.clone.clone.1.clone.1 | loop fusion | flops 369098752 | bytes 16844800 | tf_op jit(solution)/shard_map/while/body/eval_jaxpr/dot_general | solution.py:32
  115.0 8.8 fusion.122
  124.0 3.1 dynamic_update_slice.9
  127.3 91.7 %fusion.121 = bf16[512,16384]{1,0:T(8,128)(2,1)} fusion(s32[16384]{0:T(1024)S(1)} %add_select_fusion.18, s32[512]{0:T(512)S(1)} %add_select_fusion.19), kind=kLoop, calls=%fused_computation.18.clone.clone.clone.clone.1.clone.1 | loop fusion | flops 369098752 | bytes 16844800 | tf_op jit(solution)/shard_map/while/body/eval_jaxpr/dot_general | solution.py:32
  218.9 8.8 fusion.122
  227.9 3.1 dynamic_update_slice.9
  231.1 91.7 %fusion.121 = bf16[512,16384]{1,0:T(8,128)(2,1)} fusion(s32[16384]{0:T(1024)S(1)} %add_select_fusion.18, s32[512]{0:T(512)S(1)} %add_select_fusion.19), kind=kLoop, calls=%fused_computation.18.clone.clone.clone.clone.1.clone.1 | loop fusion | flops 369098752 | bytes 16844800 | tf_op jit(solution)/shard_map/while/body/eval_jaxpr/dot_general | solution.py:32
  322.8 8.8 fusion.122
  331.8 3.1 dynamic_update_slice.9
  335.0 91.7 %fusion.121 = bf16[512,16384]{1,0:T(8,128)(2,1)} fusion(s32[16384]{0:T(1024)S(1)} %add_select_fusion.18, s32[512]{0:T(512)S(1)} %add_select_fusion.19), kind=kLoop, calls=%fused_computation.18.clone.clone.clone.clone.1.clone.1 | loop fusion | flops 369098752 | bytes 16844800 | tf_op jit(solution)/shard_map/while/body/eval_jaxpr/dot_general | solution.py:32
  426.7 8.8 fusion.122
  435.7 3.1 dynamic_update_slice.9
  438.9 1.0 copy.42
  440.0 36.3 %all-reduce.3.cloned.1.call-done = f32[2048,65]{0,1:T(8,128)} async-done(((f32[2048,65]{0,1:T(8,128)}), f32[2048,65]{0,1:T(8,128)}) %all-reduce.3.cloned.1.call-update) | async-done | bytes 532496 | tf_op jit(solution)/shard_map/psum | solution.py:91
  476.3 0.9 subtract_multiply_fusion.1
  477.2 1.1 fusion.77
  478.4 381.5 %while.31 = (s32[]{:T(128)}, f32[16384,65]{0,1:T(8,128)}, s32[2048]{0:T(1024)}, s32[]{:T(128)}, bf16[2048,65]{0,1:T(8,128)(2,1)S(1)}, /*index=5*/s32[]{:T(128)}, s32[]{:T(128)}, s32[]{:T(128)}, s32[]{:T(128)}) while((s32[]{:T(128)}, f32[16384,65]{0,1:T(8,128)}, s32[2048]{0:T(1024)}, s32[]{:T(128)}, bf16[2048,65]{0,1:T(8,128)(2,1)S(1)}, ...), condition=%wide.region_4.5_spmd.clone, body=%wide.region_3.4_spmd.clone.sunk | while | flops 1461882368 | bytes 8730785 | solution.py:52
  478.6 0.9 add_select_fusion.21
  479.6 93.6 %convolution_add_fusion.2 = f32[16384,65]{0,1:T(8,128)} fusion(s32[16384]{0:T(1024)S(1)} %add_select_fusion.20, s32[512]{0:T(512)S(1)} %add_select_fusion.21, f32[16384,65]{0,1:T(8,128)} %get-tuple-element.400, pred[]{:T(512)S(6)} %compare.19, bf16[2048,65]{0,1:T(8,128)(2,1)S(1)} %get-tuple-element.412, s32[]{:T(128)S(6)} %select_n.397), kind=kOutput, calls=%fused_computation.70.clone.3 | convolution fusion | flops 1461747712 | bytes 8660997 | tf_op jit(solution)/shard_map/while/body/eval_jaxpr/dot_general | solution.py:48
  573.1 0.8 add_select_fusion.21
  574.0 94.8 %convolution_add_fusion.2 = f32[16384,65]{0,1:T(8,128)} fusion(s32[16384]{0:T(1024)S(1)} %add_select_fusion.20, s32[512]{0:T(512)S(1)} %add_select_fusion.21, f32[16384,65]{0,1:T(8,128)} %get-tuple-element.400, pred[]{:T(512)S(6)} %compare.19, bf16[2048,65]{0,1:T(8,128)(2,1)S(1)} %get-tuple-element.412, s32[]{:T(128)S(6)} %select_n.397), kind=kOutput, calls=%fused_computation.70.clone.3 | convolution fusion | flops 1461747712 | bytes 8660997 | tf_op jit(solution)/shard_map/while/body/eval_jaxpr/dot_general | solution.py:48
  668.7 0.8 add_select_fusion.21
  669.6 94.8 %convolution_add_fusion.2 = f32[16384,65]{0,1:T(8,128)} fusion(s32[16384]{0:T(1024)S(1)} %add_select_fusion.20, s32[512]{0:T(512)S(1)} %add_select_fusion.21, f32[16384,65]{0,1:T(8,128)} %get-tuple-element.400, pred[]{:T(512)S(6)} %compare.19, bf16[2048,65]{0,1:T(8,128)(2,1)S(1)} %get-tuple-element.412, s32[]{:T(128)S(6)} %select_n.397), kind=kOutput, calls=%fused_computation.70.clone.3 | convolution fusion | flops 1461747712 | bytes 8660997 | tf_op jit(solution)/shard_map/while/body/eval_jaxpr/dot_general | solution.py:48
  764.3 0.8 add_select_fusion.21
  765.2 94.8 %convolution_add_fusion.2 = f32[16384,65]{0,1:T(8,128)} fusion(s32[16384]{0:T(1024)S(1)} %add_select_fusion.20, s32[512]{0:T(512)S(1)} %add_select_fusion.21, f32[16384,65]{0,1:T(8,128)} %get-tuple-element.400, pred[]{:T(512)S(6)} %compare.19, bf16[2048,65]{0,1:T(8,128)(2,1)S(1)} %get-tuple-element.412, s32[]{:T(128)S(6)} %select_n.397), kind=kOutput, calls=%fused_computation.70.clone.3 | convolution fusion | flops 1461747712 | bytes 8660997 | tf_op jit(solution)/shard_map/while/body/eval_jaxpr/dot_general | solution.py:48
  860.0 85.3 %reduce-scatter.2.cloned.1.call-done = f32[4096,65]{0,1:T(8,128)} async-done(((f32[16384,65]{0,1:T(8,128)}), f32[4096,65]{0,1:T(8,128)}) %reduce-scatter.2.cloned.1.call-update) | async-done | bytes 1064976 | tf_op jit(solution)/shard_map/reduce_scatter | solution.py:94
  945.4 2.4 slice_add_fusion
  947.8 0.9 slice.32
  948.7 0.7 multiply_add_fusion.1
  949.4 2.2 convolution_bitcast_fusion
  951.6 1.8 fusion.78
  953.4 2.6 fusion.91
  956.0 64.8 %all-reduce = (f32[64,64]{0,1:T(8,128)S(1)}, f32[64,64]{0,1:T(8,128)S(1)}, f32[64]{0:T(128)S(1)}) all-reduce(f32[64,64]{0,1:T(8,128)S(1)} %fusion.91, f32[64,64]{0,1:T(8,128)S(1)} %fusion.78, f32[64]{0:T(128)S(1)} %convolution_bitcast_fusion), channel_id=1, replica_groups=mesh['group'=2,'rows'=4,'sec'=2,'sub'=2] {'rows','sec','sub'}, use_global_device_ids=true, to_apply=%region_7.8 | all-reduce | flops 8256 | bytes 66048 | tf_op jit(solution)/shard_map/psum | solution.py:102
  1021.0 5.8 cholesky.16
  1026.9 0.6 compare_reduce_fusion
  1027.6 0.7 fusion.80
  1028.2 4.9 custom-call.8
  1033.3 0.2 convolution_bitcast_fusion.1
  1033.4 1.9 fusion.92
  1035.3 13.1 %all_gather.6 = f32[16384]{0:T(1024)S(1)} all-gather(f32[4096]{0:T(1024)S(1)} %subtract_multiply_fusion), channel_id=1, replica_groups=mesh['group'=2,'rows'=4,'sec'=2,'sub'=2] {'rows'}, dimensions={0}, use_global_device_ids=true | all-gather | bytes 81920 | tf_op jit(solution)/shard_map/all_gather | solution.py:105
  1048.5 0.6 copy.61
  1049.1 4.5 copy.62
  (53 shorter events, 1.8 us)
Async XLA Ops:
  7.2 469.1 %all-reduce.3.cloned.1.call-start = ((), (), s32[]{:S(2)}) async-start(), calls=%async_computation.1 | async-start | bytes 1179648 | tf_op jit(solution)/shard_map/psum | solution.py:91
  23.3 453.9 %copy-start.2 = (s32[2048]{0:T(1024)S(1)}, s32[2048]{0:T(1024)}, u32[]{:S(2)}) copy-start(s32[2048]{0:T(1024)} %param.9) | copy-start | bytes 24580
  23.3 91.7 %copy-start = (bf16[16384,65]{1,0:T(8,128)(2,1)S(1)}, bf16[16384,65]{1,0:T(8,128)(2,1)}, u32[]{:S(2)}) copy-start(bf16[16384,65]{1,0:T(8,128)(2,1)} %get-tuple-element.387) | copy-start | bytes 6389764 | tf_op jit(solution)/shard_map/while
  127.2 91.8 %copy-start = (bf16[16384,65]{1,0:T(8,128)(2,1)S(1)}, bf16[16384,65]{1,0:T(8,128)(2,1)}, u32[]{:S(2)}) copy-start(bf16[16384,65]{1,0:T(8,128)(2,1)} %get-tuple-element.387) | copy-start | bytes 6389764 | tf_op jit(solution)/shard_map/while
  231.0 91.8 %copy-start = (bf16[16384,65]{1,0:T(8,128)(2,1)S(1)}, bf16[16384,65]{1,0:T(8,128)(2,1)}, u32[]{:S(2)}) copy-start(bf16[16384,65]{1,0:T(8,128)(2,1)} %get-tuple-element.387) | copy-start | bytes 6389764 | tf_op jit(solution)/shard_map/while
  334.9 91.8 %copy-start = (bf16[16384,65]{1,0:T(8,128)(2,1)S(1)}, bf16[16384,65]{1,0:T(8,128)(2,1)}, u32[]{:S(2)}) copy-start(bf16[16384,65]{1,0:T(8,128)(2,1)} %get-tuple-element.387) | copy-start | bytes 6389764 | tf_op jit(solution)/shard_map/while
  440.0 505.4 %reduce-scatter.2.cloned.1.call-start = ((), (), s32[]{:S(2)}) async-start(), calls=%async_computation.2 | async-start | bytes 5898240 | tf_op jit(solution)/shard_map/reduce_scatter | solution.py:94
  478.4 466.9 %copy-start.1 = (bf16[16384,64]{0,1:T(8,128)(2,1)S(1)}, bf16[16384,64]{0,1:T(8,128)(2,1)}, u32[]{:S(2)}) copy-start(bf16[16384,64]{0,1:T(8,128)(2,1)} %param.11) | copy-start | bytes 6291460
  860.0 188.5 %all-gather.2.cloned.1.call-start = ((), (), s32[]{:S(2)}) async-start(), calls=%async_computation.3 | async-start | bytes 5242880 | tf_op jit(solution)/shard_map/all_gather | solution.py:106
Sparse Core Ops, SparseCore 0:
  440.1 36.1 all-reduce.2
  860.1 85.2 reduce-scatter.1
  947.9 82.4 all-gather.1
where the time goes:
time: 1060 us
  matrix products  422 us (40%)
  other arithmetic  394 us (37%)
  waiting for transfers between devices  122 us (12%)
  blocking collectives  77.9 us (7%)
  local copies, waits for them, and re-layouts  29.7 us (3%)
  between operations  13.9 us (1%)
    dot_general x4, matrix products, add_block(): lax.dot_general(tab, block_mixed, (((0,), (0,)), ((), ())), preferred_ele...  378 us
    dot_general x4, other arithmetic, one_block(): jnp.dot(table_block(block_seeds, first, nfeat), stacked, preferred_elemen...  367 us
    reduce_scatter x1, waiting for transfers between devices, local(): lax.psum_scatter(partial_total, 'rows', scatter_dimension=0, tiled=True)  85.3 us
    psum x1, blocking collectives, local(): core, square, proj = lax.psum((core, square, proj), ('rows', 'sec', 'sub'))  64.8 us
    psum x1, waiting for transfers between devices, local(): margins = lax.psum(local_margins, ('sec', 'sub'))  36.3 us
    dot_general x4, matrix products, one_block(): jnp.dot(table_block(block_seeds, first, nfeat), stacked, preferred_elemen...  35.3 us
  transfers between devices with their start and end apart: 3, of which 2 were waited for; matrix products, arithmetic and copies ran while one was open for 2% of the time, Pallas kernels for 0%

commit v1 on v0

--- a/solution.py
+++ b/solution.py
@@ -88,7 +88,7 @@
     first = lax.axis_index(("sec", "sub")) * nfeat
     stacked = jnp.concatenate([weights.astype(jnp.bfloat16)[:, None], sketch], axis=1)
     local_margins = margin_rows(row_seeds, first, stacked)
-    margins = lax.psum(local_margins, ("sec", "sub"))
+    margins = jnp.sum(lax.all_gather(local_margins, ("sec", "sub")), axis=0)
     mixed = weigh(margins, labels)
     partial_total = accumulate(row_seeds, mixed, first, nfeat)
     piece = lax.psum_scatter(partial_total, "rows", scatter_dimension=0, tiled=True)

time: 1060 us -> 1050 us (level)
    psum x1 -> x0, waiting for transfers between devices: 36.3 us -> none  [local(): margins = lax.psum(local_margins, ('sec', 'sub'))]
    all_gather x0 -> x1, waiting for transfers between devices: none -> 26.9 us  [local(): margins = jnp.sum(lax.all_gather(local_margins, ('sec', 'sub')), axis=0)]
where the time goes in v1:
time: 1050 us
  matrix products  422 us (40%)
  other arithmetic  394 us (38%)
  waiting for transfers between devices  112 us (11%)
  blocking collectives  77.9 us (7%)
  local copies, waits for them, and re-layouts  29.8 us (3%)
  between operations  13.9 us (1%)
    dot_general x4, matrix products, add_block(): lax.dot_general(tab, block_mixed, (((0,), (0,)), ((), ())), preferred_ele...  378 us
    dot_general x4, other arithmetic, one_block(): jnp.dot(table_block(block_seeds, first, nfeat), stacked, preferred_elemen...  367 us
    reduce_scatter x1, waiting for transfers between devices, local(): lax.psum_scatter(partial_total, 'rows', scatter_dimension=0, tiled=True)  85.4 us
    psum x1, blocking collectives, local(): core, square, proj = lax.psum((core, square, proj), ('rows', 'sec', 'sub'))  64.8 us
    dot_general x4, matrix products, one_block(): jnp.dot(table_block(block_seeds, first, nfeat), stacked, preferred_elemen...  35.3 us
    all_gather x1, waiting for transfers between devices, local(): margins = jnp.sum(lax.all_gather(local_margins, ('sec', 'sub')), axis=0)  26.9 us
  transfers between devices with their start and end apart: 3, of which 2 were waited for; matrix products, arithmetic and copies ran while one was open for 2% of the time, Pallas kernels for 0%

profile of v1, /device:TPU:0, one launch (start us, length us, event | category | flops | bytes accessed | tf_op | source)
XLA Modules:
  0.0 1050.8 jit_solution(3230828633039124152)
XLA Ops:
  7.2 0.8 convert_element_type.47
  8.1 3.8 broadcast_in_dim.39
  11.9 4.7 copy.20
  16.7 0.7 reshape.73
  17.4 5.9 pad_maximum_fusion
  23.3 415.5 %while.30 = (s32[]{:T(128)}, f32[4,512,65]{1,0,2:T(4,128)S(1)}, s32[4,512]{1,0:T(4,128)S(1)}, s32[]{:T(128)}, bf16[16384,65]{1,0:T(8,128)(2,1)}, /*index=5*/s32[]{:T(128)}, s32[]{:T(128)}) while((s32[]{:T(128)}, f32[4,512,65]{1,0,2:T(4,128)S(1)}, s32[4,512]{1,0:T(4,128)S(1)}, s32[]{:T(128)}, bf16[16384,65]{1,0:T(8,128)(2,1)}, ...), condition=%wide.region_1.2_spmd, body=%wide.region_0.1_spmd.sunk | while | flops 1459752448 | bytes 45011060 | solution.py:36
  23.4 91.7 %fusion.121 = bf16[512,16384]{1,0:T(8,128)(2,1)} fusion(s32[16384]{0:T(1024)S(1)} %add_select_fusion.18, s32[512]{0:T(512)S(1)} %add_select_fusion.19), kind=kLoop, calls=%fused_computation.18.clone.clone.clone.clone.1.clone.1 | loop fusion | flops 369098752 | bytes 16844800 | tf_op jit(solution)/shard_map/while/body/eval_jaxpr/dot_general | solution.py:32
  115.0 8.8 fusion.122
  124.0 3.1 dynamic_update_slice.9
  127.3 91.7 %fusion.121 = bf16[512,16384]{1,0:T(8,128)(2,1)} fusion(s32[16384]{0:T(1024)S(1)} %add_select_fusion.18, s32[512]{0:T(512)S(1)} %add_select_fusion.19), kind=kLoop, calls=%fused_computation.18.clone.clone.clone.clone.1.clone.1 | loop fusion | flops 369098752 | bytes 16844800 | tf_op jit(solution)/shard_map/while/body/eval_jaxpr/dot_general | solution.py:32
  218.9 8.8 fusion.122
  227.9 3.1 dynamic_update_slice.9
  231.1 91.7 %fusion.121 = bf16[512,16384]{1,0:T(8,128)(2,1)} fusion(s32[16384]{0:T(1024)S(1)} %add_select_fusion.18, s32[512]{0:T(512)S(1)} %add_select_fusion.19), kind=kLoop, calls=%fused_computation.18.clone.clone.clone.clone.1.clone.1 | loop fusion | flops 369098752 | bytes 16844800 | tf_op jit(solution)/shard_map/while/body/eval_jaxpr/dot_general | solution.py:32
  322.8 8.8 fusion.122
  331.8 3.1 dynamic_update_slice.9
  335.0 91.7 %fusion.121 = bf16[512,16384]{1,0:T(8,128)(2,1)} fusion(s32[16384]{0:T(1024)S(1)} %add_select_fusion.18, s32[512]{0:T(512)S(1)} %add_select_fusion.19), kind=kLoop, calls=%fused_computation.18.clone.clone.clone.clone.1.clone.1 | loop fusion | flops 369098752 | bytes 16844800 | tf_op jit(solution)/shard_map/while/body/eval_jaxpr/dot_general | solution.py:32
  426.7 8.8 fusion.122
  435.7 3.1 dynamic_update_slice.9
  438.8 1.2 all_gather_reshape.3
  440.1 26.9 %all-gather.3.cloned.1.call-done = f32[4,2048,65]{1,2,0:T(8,128)} async-done(((f32[1,2048,65]{1,2,0:T(8,128)}), f32[4,2048,65]{1,2,0:T(8,128)}) %all-gather.3.cloned.1.call-update) | async-done | bytes 2129936 | tf_op jit(solution)/shard_map/all_gather | solution.py:91
  467.0 1.9 reduce_sum.9
  469.1 381.5 %while.31 = (s32[]{:T(128)}, f32[16384,65]{0,1:T(8,128)}, s32[2048]{0:T(1024)}, s32[]{:T(128)}, bf16[2048,65]{0,1:T(8,128)(2,1)S(1)}, /*index=5*/s32[]{:T(128)}, s32[]{:T(128)}, s32[]{:T(128)}, s32[]{:T(128)}) while((s32[]{:T(128)}, f32[16384,65]{0,1:T(8,128)}, s32[2048]{0:T(1024)}, s32[]{:T(128)}, bf16[2048,65]{0,1:T(8,128)(2,1)S(1)}, ...), condition=%wide.region_4.5_spmd.clone, body=%wide.region_3.4_spmd.clone.sunk | while | flops 1461882368 | bytes 8730785 | solution.py:52
  469.3 0.9 add_select_fusion.21
  470.2 93.6 %convolution_add_fusion.2 = f32[16384,65]{0,1:T(8,128)} fusion(s32[16384]{0:T(1024)S(1)} %add_select_fusion.20, s32[512]{0:T(512)S(1)} %add_select_fusion.21, f32[16384,65]{0,1:T(8,128)} %get-tuple-element.400, pred[]{:T(512)S(6)} %compare.19, bf16[2048,65]{0,1:T(8,128)(2,1)S(1)} %get-tuple-element.412, s32[]{:T(128)S(6)} %select_n.397), kind=kOutput, calls=%fused_computation.70.clone.3 | convolution fusion | flops 1461747712 | bytes 8660997 | tf_op jit(solution)/shard_map/while/body/eval_jaxpr/dot_general | solution.py:48
  563.8 0.8 add_select_fusion.21
  564.6 94.8 %convolution_add_fusion.2 = f32[16384,65]{0,1:T(8,128)} fusion(s32[16384]{0:T(1024)S(1)} %add_select_fusion.20, s32[512]{0:T(512)S(1)} %add_select_fusion.21, f32[16384,65]{0,1:T(8,128)} %get-tuple-element.400, pred[]{:T(512)S(6)} %compare.19, bf16[2048,65]{0,1:T(8,128)(2,1)S(1)} %get-tuple-element.412, s32[]{:T(128)S(6)} %select_n.397), kind=kOutput, calls=%fused_computation.70.clone.3 | convolution fusion | flops 1461747712 | bytes 8660997 | tf_op jit(solution)/shard_map/while/body/eval_jaxpr/dot_general | solution.py:48
  659.4 0.8 add_select_fusion.21
  660.2 94.8 %convolution_add_fusion.2 = f32[16384,65]{0,1:T(8,128)} fusion(s32[16384]{0:T(1024)S(1)} %add_select_fusion.20, s32[512]{0:T(512)S(1)} %add_select_fusion.21, f32[16384,65]{0,1:T(8,128)} %get-tuple-element.400, pred[]{:T(512)S(6)} %compare.19, bf16[2048,65]{0,1:T(8,128)(2,1)S(1)} %get-tuple-element.412, s32[]{:T(128)S(6)} %select_n.397), kind=kOutput, calls=%fused_computation.70.clone.3 | convolution fusion | flops 1461747712 | bytes 8660997 | tf_op jit(solution)/shard_map/while/body/eval_jaxpr/dot_general | solution.py:48
  755.0 0.8 add_select_fusion.21
  755.8 94.8 %convolution_add_fusion.2 = f32[16384,65]{0,1:T(8,128)} fusion(s32[16384]{0:T(1024)S(1)} %add_select_fusion.20, s32[512]{0:T(512)S(1)} %add_select_fusion.21, f32[16384,65]{0,1:T(8,128)} %get-tuple-element.400, pred[]{:T(512)S(6)} %compare.19, bf16[2048,65]{0,1:T(8,128)(2,1)S(1)} %get-tuple-element.412, s32[]{:T(128)S(6)} %select_n.397), kind=kOutput, calls=%fused_computation.70.clone.3 | convolution fusion | flops 1461747712 | bytes 8660997 | tf_op jit(solution)/shard_map/while/body/eval_jaxpr/dot_general | solution.py:48
  850.6 85.4 %reduce-scatter.2.cloned.1.call-done = f32[4096,65]{0,1:T(8,128)} async-done(((f32[16384,65]{0,1:T(8,128)}), f32[4096,65]{0,1:T(8,128)}) %reduce-scatter.2.cloned.1.call-update) | async-done | bytes 1064976 | tf_op jit(solution)/shard_map/reduce_scatter | solution.py:94
  936.0 2.4 slice_add_fusion
  938.5 0.9 slice.32
  939.4 0.7 multiply_add_fusion.1
  940.1 2.2 convolution_bitcast_fusion
  942.3 1.8 fusion.78
  944.1 2.6 fusion.91
  946.7 64.8 %all-reduce = (f32[64,64]{0,1:T(8,128)S(1)}, f32[64,64]{0,1:T(8,128)S(1)}, f32[64]{0:T(128)S(1)}) all-reduce(f32[64,64]{0,1:T(8,128)S(1)} %fusion.91, f32[64,64]{0,1:T(8,128)S(1)} %fusion.78, f32[64]{0:T(128)S(1)} %convolution_bitcast_fusion), channel_id=1, replica_groups=mesh['group'=2,'rows'=4,'sec'=2,'sub'=2] {'rows','sec','sub'}, use_global_device_ids=true, to_apply=%region_7.8 | all-reduce | flops 8256 | bytes 66048 | tf_op jit(solution)/shard_map/psum | solution.py:102
  1011.7 5.8 cholesky.16
  1017.6 0.6 compare_reduce_fusion
  1018.2 0.7 fusion.80
  1018.9 4.9 custom-call.8
  1023.8 0.2 convolution_bitcast_fusion.2
  1023.9 0.2 convolution_bitcast_fusion.1
  1024.1 1.9 fusion.92
  1026.0 13.1 %all_gather.10 = f32[16384]{0:T(1024)S(1)} all-gather(f32[4096]{0:T(1024)S(1)} %subtract_multiply_fusion), channel_id=1, replica_groups=mesh['group'=2,'rows'=4,'sec'=2,'sub'=2] {'rows'}, dimensions={0}, use_global_device_ids=true | all-gather | bytes 81920 | tf_op jit(solution)/shard_map/all_gather | solution.py:105
  1039.1 0.6 copy.51
  1039.8 4.5 copy.52
  (53 shorter events, 1.6 us)
Async XLA Ops:
  7.2 459.8 %all-gather.3.cloned.1.call-start = ((), (), s32[]{:S(2)}) async-start(), calls=%async_computation.1 | async-start | bytes 2949120 | tf_op jit(solution)/shard_map/all_gather | solution.py:91
  23.3 445.7 %copy-start.2 = (s32[2048]{0:T(1024)S(1)}, s32[2048]{0:T(1024)}, u32[]{:S(2)}) copy-start(s32[2048]{0:T(1024)} %param.9) | copy-start | bytes 24580
  23.3 91.7 %copy-start = (bf16[16384,65]{1,0:T(8,128)(2,1)S(1)}, bf16[16384,65]{1,0:T(8,128)(2,1)}, u32[]{:S(2)}) copy-start(bf16[16384,65]{1,0:T(8,128)(2,1)} %get-tuple-element.387) | copy-start | bytes 6389764 | tf_op jit(solution)/shard_map/while
  127.2 91.8 %copy-start = (bf16[16384,65]{1,0:T(8,128)(2,1)S(1)}, bf16[16384,65]{1,0:T(8,128)(2,1)}, u32[]{:S(2)}) copy-start(bf16[16384,65]{1,0:T(8,128)(2,1)} %get-tuple-element.387) | copy-start | bytes 6389764 | tf_op jit(solution)/shard_map/while
  231.0 91.8 %copy-start = (bf16[16384,65]{1,0:T(8,128)(2,1)S(1)}, bf16[16384,65]{1,0:T(8,128)(2,1)}, u32[]{:S(2)}) copy-start(bf16[16384,65]{1,0:T(8,128)(2,1)} %get-tuple-element.387) | copy-start | bytes 6389764 | tf_op jit(solution)/shard_map/while
  334.9 91.8 %copy-start = (bf16[16384,65]{1,0:T(8,128)(2,1)S(1)}, bf16[16384,65]{1,0:T(8,128)(2,1)}, u32[]{:S(2)}) copy-start(bf16[16384,65]{1,0:T(8,128)(2,1)} %get-tuple-element.387) | copy-start | bytes 6389764 | tf_op jit(solution)/shard_map/while
  440.0 496.0 %reduce-scatter.2.cloned.1.call-start = ((), (), s32[]{:S(2)}) async-start(), calls=%async_computation.2 | async-start | bytes 5898240 | tf_op jit(solution)/shard_map/reduce_scatter | solution.py:94
  469.1 467.0 %copy-start.1 = (bf16[16384,64]{0,1:T(8,128)(2,1)S(1)}, bf16[16384,64]{0,1:T(8,128)(2,1)}, u32[]{:S(2)}) copy-start(bf16[16384,64]{0,1:T(8,128)(2,1)} %param.11) | copy-start | bytes 6291460
  850.6 188.5 %all-gather.5.cloned.1.call-start = ((), (), s32[]{:S(2)}) async-start(), calls=%async_computation.3 | async-start | bytes 5242880 | tf_op jit(solution)/shard_map/all_gather | solution.py:106
Sparse Core Ops, SparseCore 0:
  440.2 26.7 all-gather.2
  850.7 85.2 reduce-scatter.1
  938.6 82.4 all-gather.4
